TPU v7x, 512 devices: a whole 4x4x16 slice. The times are simulated.
512 devices in a mesh: seq: 32 (over z, core), table: 16 (over x, y).
Axes of the slice: x: 4, y: 4, z: 16, core: 2. Of those that a mesh axis runs over, the one named last changes fastest.
Arguments:
- columns: bfloat16 [16, 8192, 512], P(None, 'seq', 'table'), may hold values from -6 to 6
- gaps: float32 [16, 8192], P('table', 'seq'), may hold values from 0.2 to 9830.4
- norm_in: float32 [512], replicated, may hold values from 0.1 to 1.9
- w_gate: bfloat16 [512, 1024], replicated, may hold values from -0.25 to 0.25
- w_xbc: bfloat16 [512, 1280], replicated, may hold values from -0.25 to 0.25
- w_step: bfloat16 [512, 16], replicated, may hold values from -0.25 to 0.25
- step_bias: float32 [16], replicated, may hold values from -1 to 1
- conv_weight: float32 [4, 1280], replicated, may hold values from -1 to 1
- conv_bias: float32 [1280], replicated, may hold values from -1.5 to 1.5
- rates: float32 [16], replicated, may hold values from 6.1035156e-06 to 0.04
- norm_out: float32 [1024], replicated, may hold values from 0.1 to 1.9
- w_out: bfloat16 [1024, 512], replicated, may hold values from -0.1875 to 0.1875
Outputs:
- mixed: bfloat16 [16, 8192, 512], P('table', 'seq')
All inputs are finite; a program needn't handle non-finite values.
Results may differ from a plain program's by a relative error of at most 0.02.
Values may be sent and summed in bfloat16 or wider, within the bound.
No kernel may reach another device: no remote copies, remote signals or barrier semaphores. Data moves between devices by JAX's collectives and lax.ppermute only.
A program may use at most 64 MiB of HBM per device.

v0:
```python
import jax
import jax.numpy as jnp
from jax import lax
from jax.sharding import PartitionSpec as P

BLOCK = 256
epsilon = 1e-05


def passed_along(block, axis, distance):
    devices = range(lax.axis_size(axis))
    route = [(i - distance, i) for i in devices if i - distance in devices]
    return lax.ppermute(block, axis, route)


def rms_rows(values, gain):
    return values * lax.rsqrt(jnp.mean(values * values, axis=-1, keepdims=True) + epsilon) * gain


def block_terms(cx, cb, cc, cdt, cda):
    length = cx.shape[0]
    cs = jnp.cumsum(cda, axis=0)
    scores = jnp.dot(cc, cb.T, preferred_element_type=jnp.float32)
    trail = cs.T
    diff = trail[:, :, None] - trail[:, None, :]
    rows = lax.broadcasted_iota(jnp.int32, (length, length), 0)
    cols = lax.broadcasted_iota(jnp.int32, (length, length), 1)
    factor = jnp.exp(jnp.where((rows >= cols)[None], diff, -jnp.inf))
    mix = (scores[None] * factor * cdt.T[:, None, :]).astype(jnp.bfloat16)
    y_in = jnp.einsum("hts,shp->thp", mix, cx, preferred_element_type=jnp.float32)
    weighted = ((jnp.exp(cs[-1][None, :] - cs) * cdt)[:, :, None] * cx.astype(jnp.float32)).astype(
        jnp.bfloat16
    )
    block_state = jnp.einsum("shp,sn->hpn", weighted, cb, preferred_element_type=jnp.float32)
    return (y_in, block_state, cs)


def local_pass(xs, bm, cm, steps_dt, decay):
    length, heads, head_dim = xs.shape
    state_width = bm.shape[1]
    count = length // BLOCK
    blocks = (
        xs.reshape(count, BLOCK, heads, head_dim),
        bm.reshape(count, BLOCK, state_width),
        cm.reshape(count, BLOCK, state_width),
        steps_dt.reshape(count, BLOCK, heads),
        decay.reshape(count, BLOCK, heads),
    )

    def one_block(block):
        return block_terms(block[0], block[1], block[2], block[3], block[4])

    y_in, states, cs = lax.map(one_block, blocks)
    ends = cs[:, -1, :]

    def walk(state, paired):
        return (jnp.exp(paired[0])[:, None, None] * state + paired[1], state)

    final, entries = lax.scan(walk, jnp.zeros(states.shape[1:], jnp.float32), (ends, states))
    starts = jnp.cumsum(ends, axis=0) - ends
    total = jnp.sum(ends, axis=0)
    return (y_in, cs, entries, starts, final, total)


def carried_output(cm, cs, entries, starts, incoming):
    count, length = (cs.shape[0], cs.shape[1])
    queries = cm.reshape(count, length, cm.shape[1])
    enter = (entries + jnp.exp(starts)[:, :, None, None] * incoming[None]).astype(jnp.bfloat16)
    picked = jnp.einsum("ktn,khpn->kthp", queries, enter, preferred_element_type=jnp.float32)
    return jnp.exp(cs)[..., None] * picked


GROUP = 8


def parts_of(values):
    high = values.astype(jnp.bfloat16)
    rest = values - high.astype(jnp.float32)
    middle = rest.astype(jnp.bfloat16)
    low = (rest - middle.astype(jnp.float32)).astype(jnp.bfloat16)
    return jnp.stack([high, middle, low])


def within_groups(blocks):
    count = lax.axis_size("seq") // GROUP
    groups = [[g * GROUP + i for i in range(GROUP)] for g in range(count)]
    return lax.all_to_all(
        blocks, "seq", split_axis=0, concat_axis=0, tiled=True, axis_index_groups=groups
    )


def with_decay(state, logs):
    lead = state.shape[:-3]
    heads, head_dim, width = state.shape[-3:]
    rows = jnp.moveaxis(parts_of(logs), 0, -1).reshape(lead + (heads * 3, 1))
    rows = jnp.broadcast_to(rows, lead + (heads * 3, width))
    pad = [(0, 0)] * len(lead) + [(0, -(heads * 3) % 8), (0, 0)]
    flat = state.astype(jnp.bfloat16).reshape(lead + (heads * head_dim, width))
    return jnp.concatenate([flat, jnp.pad(rows, pad)], axis=-2)


def without_decay(block, heads):
    width = block.shape[-1]
    lead = block.shape[:-2]
    block = block.astype(jnp.float32)
    size = block.shape[-2] - heads * 3 - -(heads * 3) % 8
    state = block[..., :size, :].reshape(lead + (heads, size // heads, width))
    logs = block[..., size : size + heads * 3, 0].reshape(lead + (heads, 3)).sum(-1)
    return (state, logs)


def carry_in(total, final):
    heads, head_dim, width = final.shape
    own = heads // GROUP
    grouped = with_decay(final.reshape(GROUP, own, head_dim, width), total.reshape(GROUP, own))
    states, logs = without_decay(within_groups(grouped), own)
    prefix = [jnp.zeros_like(states[0])]
    before = [jnp.zeros_like(logs[0])]
    for member in range(GROUP):
        prefix.append(jnp.exp(logs[member])[:, None, None] * prefix[-1] + states[member])
        before.append(before[-1] + logs[member])
    block = with_decay(prefix[-1], before[-1])
    count = lax.axis_size("seq") // GROUP
    arrived = [
        without_decay(passed_along(block, "seq", GROUP * step), own) for step in range(1, count)
    ]
    enter = arrived[-1][0]
    for state, log in arrived[-2::-1]:
        enter = state + jnp.exp(log)[:, None, None] * enter
    back = jnp.stack(
        [prefix[member] + jnp.exp(before[member])[:, None, None] * enter for member in range(GROUP)]
    ).astype(jnp.bfloat16)
    return within_groups(back.reshape(GROUP, own * head_dim, width)).reshape(heads, head_dim, width)


def local(
    columns,
    gaps,
    norm_in,
    w_gate,
    w_xbc,
    w_step,
    step_bias,
    conv_weight,
    conv_bias,
    rates,
    norm_out,
    w_out,
):
    inner = w_gate.shape[1]
    heads = w_step.shape[1]
    head_dim = inner // heads
    state_width = (w_xbc.shape[1] - inner) // 2
    reach = conv_weight.shape[0] - 1
    normed = rms_rows(
        lax.all_to_all(columns, "table", split_axis=0, concat_axis=2, tiled=True).astype(
            jnp.float32
        ),
        norm_in,
    ).astype(jnp.bfloat16)
    gate = jnp.einsum("brd,de->bre", normed, w_gate, preferred_element_type=jnp.float32).astype(
        jnp.bfloat16
    )
    xbc = jnp.einsum("brd,de->bre", normed, w_xbc, preferred_element_type=jnp.float32).astype(
        jnp.bfloat16
    )
    step_raw = jnp.einsum("brd,de->bre", normed, w_step, preferred_element_type=jnp.float32)
    gate, xbc, step_raw, normed = (gate, xbc, step_raw, normed)
    hists, length = (xbc.shape[0], xbc.shape[1])
    rim = passed_along(xbc[:, length - reach :, :], "seq", 1)
    padded = jnp.concatenate([rim, xbc], axis=1).astype(jnp.float32)
    conv = conv_bias + conv_weight[0] * padded[:, 0:length]
    for offset in range(1, reach + 1):
        conv = conv + conv_weight[offset] * padded[:, offset : offset + length]
    act = jax.nn.silu(conv).astype(jnp.bfloat16)
    xs = act[:, :, :inner].reshape(hists, length, heads, head_dim)
    bm = act[:, :, inner : inner + state_width]
    cm = act[:, :, inner + state_width :]
    steps_dt = jax.nn.softplus(step_raw + step_bias)
    decay = -rates * steps_dt * gaps[:, :, None]
    y_in, cs, entries, starts, final, total = jax.vmap(local_pass)(xs, bm, cm, steps_dt, decay)
    incoming = carry_in(total[0], final[0])[None].astype(jnp.float32)
    state_terms = jax.vmap(carried_output)(cm, cs, entries, starts, incoming)
    y = (y_in + state_terms).reshape(hists, length, inner)
    gated = y * jax.nn.silu(gate.astype(jnp.float32))
    out_normed = rms_rows(gated, norm_out).astype(jnp.bfloat16)
    return jnp.einsum("bri,id->brd", out_normed, w_out, preferred_element_type=jnp.float32).astype(
        jnp.bfloat16
    )


def solution(mesh):
    in_specs = (
        P(None, "seq", "table"),
        P("table", "seq"),
        P(),
        P(),
        P(),
        P(),
        P(),
        P(),
        P(),
        P(),
        P(),
        P(),
    )
    out_specs = P("table", "seq", None)
    return jax.shard_map(local, mesh=mesh, in_specs=in_specs, out_specs=out_specs, check_vma=False)
```

profile of v0, /device:TPU:1, one launch (start us, length us, event | category | flops | bytes accessed | tf_op | source)
XLA Modules:
  0.0 95.5 jit_solution(16573989811518434025)
XLA Ops:
  0.0 7.7 %all-to-all-start = ((bf16[16,256,32]{1,2,0:T(8,128)(2,1)}), bf16[16,256,32]{1,2,0:T(8,128)(2,1)S(1)}, u32[]{:S(2)}, u32[]{:S(2)}) async-start(bf16[16,256,32]{1,2,0:T(8,128)(2,1)} %param.12), calls=%async_computation | async-start | bytes 524288 | tf_op jit(solution)/shard_map/all_to_all | solution.py:156
  7.8 0.7 neg.18
  8.4 0.9 slice_reduce_fusion.6
  9.4 5.8 %all-to-all-done = bf16[16,256,32]{1,2,0:T(8,128)(2,1)S(1)} async-done(((bf16[16,256,32]{1,2,0:T(8,128)(2,1)}), bf16[16,256,32]{1,2,0:T(8,128)(2,1)S(1)}, u32[]{:S(2)}, u32[]{:S(2)}) %all-to-all-start) | async-done | bytes 262176 | tf_op jit(solution)/shard_map/all_to_all | solution.py:156
  15.3 0.8 fusion.22
  16.1 0.2 compare_select_fusion
  16.4 0.6 reduce-window.6
  16.9 0.2 slice_reduce_fusion
  17.3 0.6 exponential_bitcast_fusion
  18.0 0.2 slice_reduce_fusion.1
  18.2 0.5 fusion
  18.8 5.5 %collective-permute-start = (bf16[1,3,1280]{2,1,0:T(4,128)(2,1)S(1)}, bf16[1,3,1280]{2,1,0:T(4,128)(2,1)S(1)}, u32[]{:S(2)}, u32[]{:S(2)}) collective-permute-start(bf16[1,3,1280]{2,1,0:T(4,128)(2,1)S(1)} %slice.182), channel_id=1, source_target_pairs={{0,16},{16,32},{32,48},{48,64},{64,80},{80,96},{96,112},{112,128},... | collective-permute-start | bytes 23048 | tf_op jit(solution)/shard_map/ppermute | solution.py:13
  24.3 0.2 exponential_reduce_fusion
  24.7 1.1 %mul.674 = f32[256,16,64]{0,2,1:T(8,128)} broadcast(f32[256,16]{0,1:T(8,128)S(1)} %fusion.60), dimensions={0,1} | broadcast | bytes 1064960 | tf_op jit(solution)/shard_map/vmap()/while/body/eval_jaxpr/mul | solution.py:31
  25.8 1.6 %copy.82 = f32[1,256,1024]{2,1,0:T(8,128)S(1)} copy(f32[1,256,1024]{1,2,0:T(8,128)} %bitcast.196) | data formatting | bytes 2097152 | tf_op jit(solution)/shard_map/vmap()/while/body/eval_jaxpr/mul | solution.py:31
  27.7 0.4 copy-done.4
  28.0 0.8 multiply_convert_fusion.4
  28.9 0.9 multiply_convert_fusion.6
  29.8 1.2 %copy.83 = bf16[1,256,1024]{1,2,0:T(8,128)(2,1)S(1)} copy(bf16[1,256,1024]{2,1,0:T(8,128)(2,1)} %multiply_convert_fusion.6) | data formatting | bytes 1048576 | tf_op jit(solution)/shard_map/vmap()/while/body/eval_jaxpr/convert_element_type | solution.py:31
  31.1 0.3 fusion.14
  31.5 16.6 %all_to_all.19 = bf16[8,136,128]{2,1,0:T(8,128)(2,1)S(1)} all-to-all(bf16[8,136,128]{2,1,0:T(8,128)(2,1)S(1)} %fusion.25), channel_id=1, replica_groups={{0,16,32,48,64,80,96,112},{128,144,160,176,192,208,224,240},{256,272,28..., dimensions={0} | all-to-all | bytes 557056 | tf_op jit(solution)/shard_map/all_to_all | solution.py:87
  48.4 0.4 exponential_reduce_fusion.1
  50.2 0.2 fusion.29
  50.5 8.8 %collective-permute-start.1 = (bf16[136,128]{1,0:T(8,128)(2,1)S(1)}, bf16[136,128]{1,0:T(8,128)(2,1)S(1)}, u32[]{:S(2)}, u32[]{:S(2)}) collective-permute-start(bf16[136,128]{1,0:T(8,128)(2,1)S(1)} %pad_maximum_fusion), channel_id=1, source_target_pairs={{0,128},{16,144},{32,160},{48,176},{64,192},{80,208},{96,224},{112... | collective-permute-start | bytes 104456 | tf_op jit(solution)/shard_map/ppermute | solution.py:13
  59.3 5.4 %collective-permute-start.2 = (bf16[136,128]{1,0:T(8,128)(2,1)S(1)}, bf16[136,128]{1,0:T(8,128)(2,1)S(1)}, u32[]{:S(2)}, u32[]{:S(2)}) collective-permute-start(bf16[136,128]{1,0:T(8,128)(2,1)S(1)} %pad_maximum_fusion), channel_id=1, source_target_pairs={{0,256},{16,272},{32,288},{48,304},{64,320},{80,336},{96,352},{112... | collective-permute-start | bytes 104456 | tf_op jit(solution)/shard_map/ppermute | solution.py:13
  64.7 1.3 %collective-permute-start.3 = (bf16[136,128]{1,0:T(8,128)(2,1)S(1)}, bf16[136,128]{1,0:T(8,128)(2,1)S(1)}, u32[]{:S(2)}, u32[]{:S(2)}) collective-permute-start(bf16[136,128]{1,0:T(8,128)(2,1)S(1)} %pad_maximum_fusion), channel_id=1, source_target_pairs={{0,384},{16,400},{32,416},{48,432},{64,448},{80,464},{96,480},{112... | collective-permute-start | bytes 104456 | tf_op jit(solution)/shard_map/ppermute | solution.py:13
  68.1 2.2 %collective-permute-done.3 = bf16[136,128]{1,0:T(8,128)(2,1)S(1)} collective-permute-done((bf16[136,128]{1,0:T(8,128)(2,1)S(1)}, bf16[136,128]{1,0:T(8,128)(2,1)S(1)}, u32[]{:S(2)}, u32[]{:S(2)}) %collective-permute-start.3) | collective-permute-done | bytes 34848 | tf_op jit(solution)/shard_map/ppermute | solution.py:13
  70.3 0.7 bitcast_dynamic-update-slice_fusion
  71.0 0.7 fusion.53
  71.7 0.7 fusion.54
  72.5 0.7 fusion.55
  73.2 0.7 fusion.56
  73.9 0.7 fusion.57
  74.7 0.7 fusion.58
  75.4 0.7 fusion.59
  76.1 4.0 %all-to-all-start.2 = ((bf16[8,128,128]{2,1,0:T(8,128)(2,1)}), bf16[8,128,128]{2,1,0:T(8,128)(2,1)S(1)}, u32[]{:S(2)}, u32[]{:S(2)}) async-start(bf16[8,128,128]{2,1,0:T(8,128)(2,1)} %fusion.59), calls=%async_computation.2 | async-start | bytes 524288 | tf_op jit(solution)/shard_map/all_to_all | solution.py:87
  80.1 0.6 iota_compare_fusion.1
  80.9 0.7 mul.667
  81.6 0.6 bitcast_add_fusion.14
  82.2 0.2 copy.77
  82.5 0.2 fusion.46
  82.7 3.2 %fusion.8 = f32[256,16,64]{0,2,1:T(8,128)} fusion(bf16[256,16,64]{0,2,1:T(8,128)(2,1)S(1)} %bitcast.200, f32[16,256]{1,0:T(8,128)S(1)} %bitcast.201, f32[16,256]{1,0:T(8,128)} %bitcast_add_fusion.14, f32[256,256]{1,0:T(8,128)S(1)} %fusion.46, pred[256,256]{1,0:T(8,128)(4,1)} %iota_compare_fusion.1), kind=kOutput, calls=%fused_computation.10 | convolution fusion | flops 139460608 | bytes 1933312 | tf_op jit(solution)/shard_map/vmap()/while/body/eval_jaxpr/hts,shp->thp/dot_general | solution.py:30
  85.9 3.0 %all-to-all-done.2 = bf16[8,128,128]{2,1,0:T(8,128)(2,1)S(1)} async-done(((bf16[8,128,128]{2,1,0:T(8,128)(2,1)}), bf16[8,128,128]{2,1,0:T(8,128)(2,1)S(1)}, u32[]{:S(2)}, u32[]{:S(2)}) %all-to-all-start.2) | async-done | bytes 262176 | tf_op jit(solution)/shard_map/all_to_all | solution.py:87
  88.8 0.2 multiply_convert_fusion.8
  89.0 1.5 %fusion.9 = f32[256,16,64]{0,2,1:T(8,128)S(1)} fusion(f32[256,16,64]{0,2,1:T(8,128)} %fusion.8, bf16[16,64,128]{2,1,0:T(8,128)(2,1)S(1)} %bitcast.198, f32[256,16]{0,1:T(8,128)} %get-tuple-element.68, bf16[1,256,1280]{2,1,0:T(8,128)(2,1)S(1)} %multiply_convert_fusion.4), kind=kOutput, calls=%fused_computation.12 | convolution fusion | flops 67633152 | bytes 2441216 | tf_op jit(solution)/shard_map/vmap(ktn,khpn->kthp)/dot_general | solution.py:69
  90.6 1.3 %copy.89 = f32[256,1024]{1,0:T(8,128)} copy(f32[256,1024]{0,1:T(8,128)S(1)} %bitcast.195) | data formatting | bytes 2097152 | tf_op jit(solution)/shard_map/reshape | solution.py:184
  91.9 2.3 %multiply_reduce_fusion = (f32[256]{0:T(256)S(1)}, f32[256,1024]{1,0:T(8,128)S(1)}) fusion(f32[256,1024]{1,0:T(8,128)} %copy.89, bf16[256,512]{0,1:T(8,128)(2,1)S(1)} %fusion.22, bf16[512,1024]{1,0:T(8,128)(2,1)} %param.15), kind=kOutput, calls=%fused_computation.35 | convolution fusion | flops 270794496 | bytes 3408896 | tf_op jit(solution)/shard_map/brd,de->bre/dot_general | solution.py:161
  94.3 1.2 %fusion.15 = bf16[1,256,512]{2,1,0:T(8,128)(2,1)} fusion(bf16[1024,512]{1,0:T(8,128)(2,1)S(1)} %copy-done.1, f32[256,1024]{1,0:T(8,128)S(1)} %get-tuple-element.88, f32[1024]{0:T(1024)S(1)} %copy-done.5, f32[256]{0:T(256)S(1)} %add_rsqrt_fusion), kind=kOutput, calls=%fused_computation.28 | convolution fusion | flops 269352960 | bytes 2364416 | tf_op jit(solution)/shard_map/bri,id->brd/dot_general | solution.py:187
  (98 shorter events, 5.2 us)
Async XLA Ops:
  0.0 18.2 %copy-start = (bf16[512,1280]{1,0:T(8,128)(2,1)S(1)}, bf16[512,1280]{1,0:T(8,128)(2,1)}, u32[]{:S(2)}) copy-start(bf16[512,1280]{1,0:T(8,128)(2,1)} %param.16) | copy-start | bytes 3932164
  0.0 16.1 %copy-start.3 = (bf16[512,16]{0,1:T(8,128)(2,1)S(1)}, bf16[512,16]{0,1:T(8,128)(2,1)}, u32[]{:S(2)}) copy-start(bf16[512,16]{0,1:T(8,128)(2,1)} %param.17) | copy-start | bytes 49156
  0.0 16.1 %copy-start.7 = (f32[16]{0:T(128)S(1)}, f32[16]{0:T(128)}, u32[]{:S(2)}) copy-start(f32[16]{0:T(128)} %param.18) | copy-start | bytes 196
  0.0 16.3 %copy-start.6 = (f32[1,256]{1,0:T(1,128)S(1)}, f32[1,256]{1,0:T(1,128)}, u32[]{:S(2)}) copy-start(f32[1,256]{1,0:T(1,128)} %param.13) | copy-start | bytes 3076
  0.0 15.1 %all-to-all-start = ((bf16[16,256,32]{1,2,0:T(8,128)(2,1)}), bf16[16,256,32]{1,2,0:T(8,128)(2,1)S(1)}, u32[]{:S(2)}, u32[]{:S(2)}) async-start(bf16[16,256,32]{1,2,0:T(8,128)(2,1)} %param.12), calls=%async_computation | async-start | bytes 524288 | tf_op jit(solution)/shard_map/all_to_all | solution.py:156
  18.8 8.8 %collective-permute-start = (bf16[1,3,1280]{2,1,0:T(4,128)(2,1)S(1)}, bf16[1,3,1280]{2,1,0:T(4,128)(2,1)S(1)}, u32[]{:S(2)}, u32[]{:S(2)}) collective-permute-start(bf16[1,3,1280]{2,1,0:T(4,128)(2,1)S(1)} %slice.182), channel_id=1, source_target_pairs={{0,16},{16,32},{32,48},{48,64},{64,80},{80,96},{96,112},{112,128},... | collective-permute-start | bytes 23048 | tf_op jit(solution)/shard_map/ppermute | solution.py:13
  27.3 0.7 copy-start.4
  50.5 16.6 %collective-permute-start.1 = (bf16[136,128]{1,0:T(8,128)(2,1)S(1)}, bf16[136,128]{1,0:T(8,128)(2,1)S(1)}, u32[]{:S(2)}, u32[]{:S(2)}) collective-permute-start(bf16[136,128]{1,0:T(8,128)(2,1)S(1)} %pad_maximum_fusion), channel_id=1, source_target_pairs={{0,128},{16,144},{32,160},{48,176},{64,192},{80,208},{96,224},{112... | collective-permute-start | bytes 104456 | tf_op jit(solution)/shard_map/ppermute | solution.py:13
  59.3 7.9 %collective-permute-start.2 = (bf16[136,128]{1,0:T(8,128)(2,1)S(1)}, bf16[136,128]{1,0:T(8,128)(2,1)S(1)}, u32[]{:S(2)}, u32[]{:S(2)}) collective-permute-start(bf16[136,128]{1,0:T(8,128)(2,1)S(1)} %pad_maximum_fusion), channel_id=1, source_target_pairs={{0,256},{16,272},{32,288},{48,304},{64,320},{80,336},{96,352},{112... | collective-permute-start | bytes 104456 | tf_op jit(solution)/shard_map/ppermute | solution.py:13
  64.7 5.6 %collective-permute-start.3 = (bf16[136,128]{1,0:T(8,128)(2,1)S(1)}, bf16[136,128]{1,0:T(8,128)(2,1)S(1)}, u32[]{:S(2)}, u32[]{:S(2)}) collective-permute-start(bf16[136,128]{1,0:T(8,128)(2,1)S(1)} %pad_maximum_fusion), channel_id=1, source_target_pairs={{0,384},{16,400},{32,416},{48,432},{64,448},{80,464},{96,480},{112... | collective-permute-start | bytes 104456 | tf_op jit(solution)/shard_map/ppermute | solution.py:13
  76.1 12.7 %all-to-all-start.2 = ((bf16[8,128,128]{2,1,0:T(8,128)(2,1)}), bf16[8,128,128]{2,1,0:T(8,128)(2,1)S(1)}, u32[]{:S(2)}, u32[]{:S(2)}) async-start(bf16[8,128,128]{2,1,0:T(8,128)(2,1)} %fusion.59), calls=%async_computation.2 | async-start | bytes 524288 | tf_op jit(solution)/shard_map/all_to_all | solution.py:87
  82.6 6.2 %copy-start.2 = (f32[8,128]{1,0:T(8,128)S(1)}, f32[8,128]{1,0:T(8,128)}, u32[]{:S(2)}) copy-start(f32[8,128]{1,0:T(8,128)} %mul.667) | copy-start | bytes 12292
  91.9 2.4 %copy-start.1 = (bf16[1024,512]{1,0:T(8,128)(2,1)S(1)}, bf16[1024,512]{1,0:T(8,128)(2,1)}, u32[]{:S(2)}) copy-start(bf16[1024,512]{1,0:T(8,128)(2,1)} %param.23) | copy-start | bytes 3145732
  91.9 2.4 %copy-start.5 = (f32[1024]{0:T(1024)S(1)}, f32[1024]{0:T(1024)}, u32[]{:S(2)}) copy-start(f32[1024]{0:T(1024)} %param.22) | copy-start | bytes 12292
where the time goes:
time: 96.2 us; the launch traced here: 95.5 us
  starting transfers between devices  32.7 us (34%)
  blocking collectives  16.6 us (17%)
  other arithmetic  13.6 us (14%)
  local copies, waits for them, and re-layouts  11.8 us (12%)
  waiting for transfers between devices  11 us (11%)
  matrix products  9.44 us (10%)
    ppermute x4, starting transfers between devices, passed_along(): return lax.ppermute(block, axis, route)  21 us
    all_to_all x1, blocking collectives, within_groups(): lax.all_to_all(blocks, 'seq', split_axis=0, concat_axis=0, tiled=True, ax...  16.6 us
    all_to_all x1, starting transfers between devices, local(): lax.all_to_all(columns, 'table', split_axis=0, concat_axis=2, tiled=True)  7.73 us
    all_to_all x1, waiting for transfers between devices, local(): lax.all_to_all(columns, 'table', split_axis=0, concat_axis=2, tiled=True)  5.79 us
    unnamed x7, other arithmetic  5.08 us
    all_to_all x1, starting transfers between devices, within_groups(): lax.all_to_all(blocks, 'seq', split_axis=0, concat_axis=0, tiled=True, ax...  3.98 us
    dot_general x1, matrix products, block_terms(): jnp.einsum('hts,shp->thp', mix, cx, preferred_element_type=jnp.float32)  3.2 us
    all_to_all x1, waiting for transfers between devices, within_groups(): lax.all_to_all(blocks, 'seq', split_axis=0, concat_axis=0, tiled=True, ax...  2.97 us
  transfers between devices with their start and end apart: 6, of which 3 were waited for; matrix products, arithmetic and copies ran while one was open for 13% of the time, Pallas kernels for 0%

commit v1 on v0

--- a/solution.py
+++ b/solution.py
@@ -153,9 +153,12 @@
     state_width = (w_xbc.shape[1] - inner) // 2
     reach = conv_weight.shape[0] - 1
     normed = rms_rows(
-        lax.all_to_all(columns, "table", split_axis=0, concat_axis=2, tiled=True).astype(
-            jnp.float32
-        ),
+        jnp.concatenate(
+            lax.all_to_all(
+                jnp.stack(jnp.split(columns, lax.axis_size("table"), axis=0)), "table", 0, 0
+            ),
+            axis=2,
+        ).astype(jnp.float32),
         norm_in,
     ).astype(jnp.bfloat16)
     gate = jnp.einsum("brd,de->bre", normed, w_gate, preferred_element_type=jnp.float32).astype(

time: 96.2 us -> 118 us (1.23); the launches traced: 95.5 us -> 116 us
  local copies, waits for them, and re-layouts: 11.8 us -> 33.1 us
    unnamed x16 -> x33, local copies, waits for them, and re-layouts: 0.38 us -> 20.3 us
    another operation x6 -> x7, local copies, waits for them, and re-layouts: 0.36 us -> 1.69 us  [the longest x1 1.32 us: local(): jnp.stack(jnp.split(columns, lax.axis_size('table'), axis=0))]
  transfers between devices with their start and end apart: 6 -> 6, of which waited for: 3 -> 3; matrix products, arithmetic and copies ran while one was open for 13% -> 11% of each run, Pallas kernels for 0% -> 0%
where the time goes in v1:
time: 118 us; the launch traced here: 116 us
  local copies, waits for them, and re-layouts  33.1 us (28%)
  starting transfers between devices  32.6 us (28%)
  blocking collectives  16.6 us (14%)
  other arithmetic  12.9 us (11%)
  waiting for transfers between devices  11 us (9%)
  matrix products  9.43 us (8%)
    ppermute x4, starting transfers between devices, passed_along(): return lax.ppermute(block, axis, route)  21 us
    unnamed x33, local copies, waits for them, and re-layouts  20.3 us
    all_to_all x1, blocking collectives, within_groups(): lax.all_to_all(blocks, 'seq', split_axis=0, concat_axis=0, tiled=True, ax...  16.6 us
    all_to_all x1, starting transfers between devices, local(): lax.all_to_all(jnp.stack(jnp.split(columns, lax.axis_size('table'), axis=...  7.58 us
    all_to_all x1, waiting for transfers between devices, local(): lax.all_to_all(jnp.stack(jnp.split(columns, lax.axis_size('table'), axis=...  5.79 us
    unnamed x7, other arithmetic  5.08 us
    all_to_all x1, starting transfers between devices, within_groups(): lax.all_to_all(blocks, 'seq', split_axis=0, concat_axis=0, tiled=True, ax...  3.98 us
    dot_general x1, matrix products, block_terms(): jnp.einsum('hts,shp->thp', mix, cx, preferred_element_type=jnp.float32)  3.21 us
  transfers between devices with their start and end apart: 6, of which 3 were waited for; matrix products, arithmetic and copies ran while one was open for 11% of the time, Pallas kernels for 0%

profile of v1, /device:TPU:1, one launch (start us, length us, event | category | flops | bytes accessed | tf_op | source)
XLA Modules:
  0.0 115.9 jit_solution(3067642514187429369)
XLA Ops:
  0.0 1.4 %constant_dynamic-update-slice_fusion.15 = bf16[16,1,256,32]{2,3,1,0:T(8,128)(2,1)} fusion(bf16[16,256,32]{1,2,0:T(8,128)(2,1)} %param.12), kind=kLoop, calls=%fused_computation.113 | loop fusion | bytes 32768
  1.5 1.3 %constant_dynamic-update-slice_fusion.14 = bf16[16,1,256,32]{2,3,1,0:T(8,128)(2,1)} fusion(bf16[16,1,256,32]{2,3,1,0:T(8,128)(2,1)} %constant_dynamic-update-slice_fusion.15, bf16[16,256,32]{1,2,0:T(8,128)(2,1)} %param.12), kind=kLoop, calls=%fused_computation.112 | loop fusion | bytes 32768
  2.8 1.3 %constant_dynamic-update-slice_fusion.13 = bf16[16,1,256,32]{2,3,1,0:T(8,128)(2,1)} fusion(bf16[16,1,256,32]{2,3,1,0:T(8,128)(2,1)} %constant_dynamic-update-slice_fusion.14, bf16[16,256,32]{1,2,0:T(8,128)(2,1)} %param.12), kind=kLoop, calls=%fused_computation.111 | loop fusion | bytes 32768
  4.1 1.3 %constant_dynamic-update-slice_fusion.12 = bf16[16,1,256,32]{2,3,1,0:T(8,128)(2,1)} fusion(bf16[16,1,256,32]{2,3,1,0:T(8,128)(2,1)} %constant_dynamic-update-slice_fusion.13, bf16[16,256,32]{1,2,0:T(8,128)(2,1)} %param.12), kind=kLoop, calls=%fused_computation.110 | loop fusion | bytes 32768
  5.4 1.3 %constant_dynamic-update-slice_fusion.11 = bf16[16,1,256,32]{2,3,1,0:T(8,128)(2,1)} fusion(bf16[16,1,256,32]{2,3,1,0:T(8,128)(2,1)} %constant_dynamic-update-slice_fusion.12, bf16[16,256,32]{1,2,0:T(8,128)(2,1)} %param.12), kind=kLoop, calls=%fused_computation.109 | loop fusion | bytes 32768
  6.7 1.3 %constant_dynamic-update-slice_fusion.10 = bf16[16,1,256,32]{2,3,1,0:T(8,128)(2,1)} fusion(bf16[16,1,256,32]{2,3,1,0:T(8,128)(2,1)} %constant_dynamic-update-slice_fusion.11, bf16[16,256,32]{1,2,0:T(8,128)(2,1)} %param.12), kind=kLoop, calls=%fused_computation.108 | loop fusion | bytes 32768
  8.1 1.3 %constant_dynamic-update-slice_fusion.9 = bf16[16,1,256,32]{2,3,1,0:T(8,128)(2,1)} fusion(bf16[16,1,256,32]{2,3,1,0:T(8,128)(2,1)} %constant_dynamic-update-slice_fusion.10, bf16[16,256,32]{1,2,0:T(8,128)(2,1)} %param.12), kind=kLoop, calls=%fused_computation.107 | loop fusion | bytes 32768
  9.4 1.3 %constant_dynamic-update-slice_fusion.8 = bf16[16,1,256,32]{2,3,1,0:T(8,128)(2,1)} fusion(bf16[16,1,256,32]{2,3,1,0:T(8,128)(2,1)} %constant_dynamic-update-slice_fusion.9, bf16[16,256,32]{1,2,0:T(8,128)(2,1)} %param.12), kind=kLoop, calls=%fused_computation.106 | loop fusion | bytes 32768
  10.7 1.3 %constant_dynamic-update-slice_fusion.7 = bf16[16,1,256,32]{2,3,1,0:T(8,128)(2,1)} fusion(bf16[16,1,256,32]{2,3,1,0:T(8,128)(2,1)} %constant_dynamic-update-slice_fusion.8, bf16[16,256,32]{1,2,0:T(8,128)(2,1)} %param.12), kind=kLoop, calls=%fused_computation.105 | loop fusion | bytes 32768
  12.0 1.3 %constant_dynamic-update-slice_fusion.6 = bf16[16,1,256,32]{2,3,1,0:T(8,128)(2,1)} fusion(bf16[16,1,256,32]{2,3,1,0:T(8,128)(2,1)} %constant_dynamic-update-slice_fusion.7, bf16[16,256,32]{1,2,0:T(8,128)(2,1)} %param.12), kind=kLoop, calls=%fused_computation.104 | loop fusion | bytes 32768
  13.4 1.3 %constant_dynamic-update-slice_fusion.5 = bf16[16,1,256,32]{2,3,1,0:T(8,128)(2,1)} fusion(bf16[16,1,256,32]{2,3,1,0:T(8,128)(2,1)} %constant_dynamic-update-slice_fusion.6, bf16[16,256,32]{1,2,0:T(8,128)(2,1)} %param.12), kind=kLoop, calls=%fused_computation.103 | loop fusion | bytes 32768
  14.7 1.3 %constant_dynamic-update-slice_fusion.4 = bf16[16,1,256,32]{2,3,1,0:T(8,128)(2,1)} fusion(bf16[16,1,256,32]{2,3,1,0:T(8,128)(2,1)} %constant_dynamic-update-slice_fusion.5, bf16[16,256,32]{1,2,0:T(8,128)(2,1)} %param.12), kind=kLoop, calls=%fused_computation.102 | loop fusion | bytes 32768
  16.0 1.3 %constant_dynamic-update-slice_fusion.3 = bf16[16,1,256,32]{2,3,1,0:T(8,128)(2,1)} fusion(bf16[16,1,256,32]{2,3,1,0:T(8,128)(2,1)} %constant_dynamic-update-slice_fusion.4, bf16[16,256,32]{1,2,0:T(8,128)(2,1)} %param.12), kind=kLoop, calls=%fused_computation.101 | loop fusion | bytes 32768
  17.3 1.3 %constant_dynamic-update-slice_fusion.2 = bf16[16,1,256,32]{2,3,1,0:T(8,128)(2,1)} fusion(bf16[16,1,256,32]{2,3,1,0:T(8,128)(2,1)} %constant_dynamic-update-slice_fusion.3, bf16[16,256,32]{1,2,0:T(8,128)(2,1)} %param.12), kind=kLoop, calls=%fused_computation.100 | loop fusion | bytes 32768
  18.7 1.3 %constant_dynamic-update-slice_fusion.1 = bf16[16,1,256,32]{2,3,1,0:T(8,128)(2,1)} fusion(bf16[16,1,256,32]{2,3,1,0:T(8,128)(2,1)} %constant_dynamic-update-slice_fusion.2, bf16[16,256,32]{1,2,0:T(8,128)(2,1)} %param.12), kind=kLoop, calls=%fused_computation.99 | loop fusion | bytes 32768
  20.0 1.3 %constant_dynamic-update-slice_fusion = bf16[16,1,256,32]{2,3,1,0:T(8,128)(2,1)} fusion(bf16[16,1,256,32]{2,3,1,0:T(8,128)(2,1)} %constant_dynamic-update-slice_fusion.1, bf16[16,256,32]{1,2,0:T(8,128)(2,1)} %param.12), kind=kLoop, calls=%fused_computation.98 | loop fusion | bytes 32768 | tf_op jit(solution)/shard_map/stack | solution.py:158
  21.3 7.6 %all-to-all-start = ((bf16[16,1,256,32]{2,3,1,0:T(8,128)(2,1)}), bf16[16,1,256,32]{2,3,1,0:T(8,128)(2,1)S(1)}, u32[]{:S(2)}, u32[]{:S(2)}) async-start(bf16[16,1,256,32]{2,3,1,0:T(8,128)(2,1)} %constant_dynamic-update-slice_fusion), calls=%async_computation | async-start | bytes 524288 | tf_op jit(solution)/shard_map/all_to_all | solution.py:157
  28.9 0.7 neg.18
  29.6 0.9 slice_reduce_fusion.6
  30.5 5.8 %all-to-all-done = bf16[16,1,256,32]{2,3,1,0:T(8,128)(2,1)S(1)} async-done(((bf16[16,1,256,32]{2,3,1,0:T(8,128)(2,1)}), bf16[16,1,256,32]{2,3,1,0:T(8,128)(2,1)S(1)}, u32[]{:S(2)}, u32[]{:S(2)}) %all-to-all-start) | async-done | bytes 262176 | tf_op jit(solution)/shard_map/all_to_all | solution.py:157
  39.2 5.5 %collective-permute-start = (bf16[1,3,1280]{2,1,0:T(4,128)(2,1)S(1)}, bf16[1,3,1280]{2,1,0:T(4,128)(2,1)S(1)}, u32[]{:S(2)}, u32[]{:S(2)}) collective-permute-start(bf16[1,3,1280]{2,1,0:T(4,128)(2,1)S(1)} %slice.182), channel_id=1, source_target_pairs={{0,16},{16,32},{32,48},{48,64},{64,80},{80,96},{96,112},{112,128},... | collective-permute-start | bytes 23048 | tf_op jit(solution)/shard_map/ppermute | solution.py:13
  45.2 1.1 mul.673
  46.2 1.6 %copy.82 = f32[1,256,1024]{2,1,0:T(8,128)S(1)} copy(f32[1,256,1024]{1,2,0:T(8,128)} %bitcast.226) | data formatting | bytes 2097152 | tf_op jit(solution)/shard_map/vmap()/while/body/eval_jaxpr/mul | solution.py:31
  48.5 0.8 multiply_convert_fusion.4
  49.3 0.9 multiply_convert_fusion.6
  50.3 1.2 %copy.83 = bf16[1,256,1024]{1,2,0:T(8,128)(2,1)S(1)} copy(bf16[1,256,1024]{2,1,0:T(8,128)(2,1)} %multiply_convert_fusion.6) | data formatting | bytes 1048576 | tf_op jit(solution)/shard_map/vmap()/while/body/eval_jaxpr/convert_element_type | solution.py:31
  51.9 16.6 %all_to_all.15 = bf16[8,136,128]{2,1,0:T(8,128)(2,1)S(1)} all-to-all(bf16[8,136,128]{2,1,0:T(8,128)(2,1)S(1)} %fusion.25), channel_id=1, replica_groups={{0,16,32,48,64,80,96,112},{128,144,160,176,192,208,224,240},{256,272,28..., dimensions={0} | all-to-all | bytes 557056 | tf_op jit(solution)/shard_map/all_to_all | solution.py:87
  71.0 8.8 %collective-permute-start.1 = (bf16[136,128]{1,0:T(8,128)(2,1)S(1)}, bf16[136,128]{1,0:T(8,128)(2,1)S(1)}, u32[]{:S(2)}, u32[]{:S(2)}) collective-permute-start(bf16[136,128]{1,0:T(8,128)(2,1)S(1)} %pad_maximum_fusion), channel_id=1, source_target_pairs={{0,128},{16,144},{32,160},{48,176},{64,192},{80,208},{96,224},{112... | collective-permute-start | bytes 104456 | tf_op jit(solution)/shard_map/ppermute | solution.py:13
  79.8 5.4 %collective-permute-start.2 = (bf16[136,128]{1,0:T(8,128)(2,1)S(1)}, bf16[136,128]{1,0:T(8,128)(2,1)S(1)}, u32[]{:S(2)}, u32[]{:S(2)}) collective-permute-start(bf16[136,128]{1,0:T(8,128)(2,1)S(1)} %pad_maximum_fusion), channel_id=1, source_target_pairs={{0,256},{16,272},{32,288},{48,304},{64,320},{80,336},{96,352},{112... | collective-permute-start | bytes 104456 | tf_op jit(solution)/shard_map/ppermute | solution.py:13
  85.2 1.3 %collective-permute-start.3 = (bf16[136,128]{1,0:T(8,128)(2,1)S(1)}, bf16[136,128]{1,0:T(8,128)(2,1)S(1)}, u32[]{:S(2)}, u32[]{:S(2)}) collective-permute-start(bf16[136,128]{1,0:T(8,128)(2,1)S(1)} %pad_maximum_fusion), channel_id=1, source_target_pairs={{0,384},{16,400},{32,416},{48,432},{64,448},{80,464},{96,480},{112... | collective-permute-start | bytes 104456 | tf_op jit(solution)/shard_map/ppermute | solution.py:13
  88.6 2.2 %collective-permute-done.3 = bf16[136,128]{1,0:T(8,128)(2,1)S(1)} collective-permute-done((bf16[136,128]{1,0:T(8,128)(2,1)S(1)}, bf16[136,128]{1,0:T(8,128)(2,1)S(1)}, u32[]{:S(2)}, u32[]{:S(2)}) %collective-permute-start.3) | collective-permute-done | bytes 34848 | tf_op jit(solution)/shard_map/ppermute | solution.py:13
  90.8 0.7 constant_dynamic-update-slice_fusion.23
  91.5 0.7 constant_dynamic-update-slice_fusion.22
  92.2 0.7 constant_dynamic-update-slice_fusion.21
  92.9 0.7 constant_dynamic-update-slice_fusion.20
  93.7 0.7 constant_dynamic-update-slice_fusion.19
  94.4 0.7 constant_dynamic-update-slice_fusion.18
  95.1 0.7 constant_dynamic-update-slice_fusion.17
  95.8 0.7 constant_dynamic-update-slice_fusion.16
  96.6 4.0 %all-to-all-start.2 = ((bf16[8,128,128]{2,1,0:T(8,128)(2,1)}), bf16[8,128,128]{2,1,0:T(8,128)(2,1)S(1)}, u32[]{:S(2)}, u32[]{:S(2)}) async-start(bf16[8,128,128]{2,1,0:T(8,128)(2,1)} %constant_dynamic-update-slice_fusion.16), calls=%async_computation.2 | async-start | bytes 524288 | tf_op jit(solution)/shard_map/all_to_all | solution.py:87
  100.6 0.6 iota_compare_fusion.1
  101.4 0.7 mul.666
  103.1 3.2 %fusion.8 = f32[256,16,64]{0,2,1:T(8,128)} fusion(bf16[256,16,64]{0,2,1:T(8,128)(2,1)S(1)} %bitcast.230, f32[16,256]{1,0:T(8,128)S(1)} %bitcast.231, f32[16,256]{1,0:T(8,128)} %bitcast_add_fusion.14, f32[256,256]{1,0:T(8,128)S(1)} %fusion.46, pred[256,256]{1,0:T(8,128)(4,1)} %iota_compare_fusion.1), kind=kOutput, calls=%fused_computation.10 | convolution fusion | flops 139460608 | bytes 1933312 | tf_op jit(solution)/shard_map/vmap()/while/body/eval_jaxpr/hts,shp->thp/dot_general | solution.py:30
  106.3 3.0 %all-to-all-done.2 = bf16[8,128,128]{2,1,0:T(8,128)(2,1)S(1)} async-done(((bf16[8,128,128]{2,1,0:T(8,128)(2,1)}), bf16[8,128,128]{2,1,0:T(8,128)(2,1)S(1)}, u32[]{:S(2)}, u32[]{:S(2)}) %all-to-all-start.2) | async-done | bytes 262176 | tf_op jit(solution)/shard_map/all_to_all | solution.py:87
  109.5 1.5 %fusion.9 = f32[256,16,64]{0,2,1:T(8,128)S(1)} fusion(f32[256,16,64]{0,2,1:T(8,128)} %fusion.8, bf16[16,64,128]{2,1,0:T(8,128)(2,1)S(1)} %bitcast.228, f32[256,16]{0,1:T(8,128)} %get-tuple-element.68, bf16[1,256,1280]{2,1,0:T(8,128)(2,1)S(1)} %multiply_convert_fusion.4), kind=kOutput, calls=%fused_computation.12 | convolution fusion | flops 67633152 | bytes 2441216 | tf_op jit(solution)/shard_map/vmap(ktn,khpn->kthp)/dot_general | solution.py:69
  111.0 1.3 %copy.89 = f32[256,1024]{1,0:T(8,128)} copy(f32[256,1024]{0,1:T(8,128)S(1)} %bitcast.225) | data formatting | bytes 2097152 | tf_op jit(solution)/shard_map/reshape | solution.py:187
  112.3 2.3 %multiply_reduce_fusion = (f32[256]{0:T(256)S(1)}, f32[256,1024]{1,0:T(8,128)S(1)}) fusion(f32[256,1024]{1,0:T(8,128)} %copy.89, bf16[256,512]{0,1:T(8,128)(2,1)S(1)} %fusion.22, bf16[512,1024]{1,0:T(8,128)(2,1)} %param.15), kind=kOutput, calls=%fused_computation.35 | convolution fusion | flops 270794496 | bytes 3408896 | tf_op jit(solution)/shard_map/brd,de->bre/dot_general | solution.py:164
  114.7 1.2 %fusion.15 = bf16[1,256,512]{2,1,0:T(8,128)(2,1)} fusion(bf16[1024,512]{1,0:T(8,128)(2,1)S(1)} %copy-done.1, f32[256,1024]{1,0:T(8,128)S(1)} %get-tuple-element.88, f32[1024]{0:T(1024)S(1)} %copy-done.5, f32[256]{0:T(256)S(1)} %add_rsqrt_fusion), kind=kOutput, calls=%fused_computation.28 | convolution fusion | flops 269352960 | bytes 2364416 | tf_op jit(solution)/shard_map/bri,id->brd/dot_general | solution.py:190
  (116 shorter events, 10.2 us)
Async XLA Ops:
  0.0 38.7 %copy-start = (bf16[512,1280]{1,0:T(8,128)(2,1)S(1)}, bf16[512,1280]{1,0:T(8,128)(2,1)}, u32[]{:S(2)}) copy-start(bf16[512,1280]{1,0:T(8,128)(2,1)} %param.16) | copy-start | bytes 3932164
  0.0 36.4 %copy-start.6 = (f32[512]{0:T(512)S(1)}, f32[512]{0:T(512)}, u32[]{:S(2)}) copy-start(f32[512]{0:T(512)} %param.14) | copy-start | bytes 6148
  0.0 36.5 %copy-start.3 = (bf16[512,16]{0,1:T(8,128)(2,1)S(1)}, bf16[512,16]{0,1:T(8,128)(2,1)}, u32[]{:S(2)}) copy-start(bf16[512,16]{0,1:T(8,128)(2,1)} %param.17) | copy-start | bytes 49156
  0.0 36.5 %copy-start.8 = (f32[16]{0:T(128)S(1)}, f32[16]{0:T(128)}, u32[]{:S(2)}) copy-start(f32[16]{0:T(128)} %param.18) | copy-start | bytes 196
  0.0 36.7 %copy-start.7 = (f32[1,256]{1,0:T(1,128)S(1)}, f32[1,256]{1,0:T(1,128)}, u32[]{:S(2)}) copy-start(f32[1,256]{1,0:T(1,128)} %param.13) | copy-start | bytes 3076
  21.3 15.0 %all-to-all-start = ((bf16[16,1,256,32]{2,3,1,0:T(8,128)(2,1)}), bf16[16,1,256,32]{2,3,1,0:T(8,128)(2,1)S(1)}, u32[]{:S(2)}, u32[]{:S(2)}) async-start(bf16[16,1,256,32]{2,3,1,0:T(8,128)(2,1)} %constant_dynamic-update-slice_fusion), calls=%async_computation | async-start | bytes 524288 | tf_op jit(solution)/shard_map/all_to_all | solution.py:157
  39.2 8.8 %collective-permute-start = (bf16[1,3,1280]{2,1,0:T(4,128)(2,1)S(1)}, bf16[1,3,1280]{2,1,0:T(4,128)(2,1)S(1)}, u32[]{:S(2)}, u32[]{:S(2)}) collective-permute-start(bf16[1,3,1280]{2,1,0:T(4,128)(2,1)S(1)} %slice.182), channel_id=1, source_target_pairs={{0,16},{16,32},{32,48},{48,64},{64,80},{80,96},{96,112},{112,128},... | collective-permute-start | bytes 23048 | tf_op jit(solution)/shard_map/ppermute | solution.py:13
  47.8 0.7 copy-start.4
  71.0 16.6 %collective-permute-start.1 = (bf16[136,128]{1,0:T(8,128)(2,1)S(1)}, bf16[136,128]{1,0:T(8,128)(2,1)S(1)}, u32[]{:S(2)}, u32[]{:S(2)}) collective-permute-start(bf16[136,128]{1,0:T(8,128)(2,1)S(1)} %pad_maximum_fusion), channel_id=1, source_target_pairs={{0,128},{16,144},{32,160},{48,176},{64,192},{80,208},{96,224},{112... | collective-permute-start | bytes 104456 | tf_op jit(solution)/shard_map/ppermute | solution.py:13
  79.8 7.9 %collective-permute-start.2 = (bf16[136,128]{1,0:T(8,128)(2,1)S(1)}, bf16[136,128]{1,0:T(8,128)(2,1)S(1)}, u32[]{:S(2)}, u32[]{:S(2)}) collective-permute-start(bf16[136,128]{1,0:T(8,128)(2,1)S(1)} %pad_maximum_fusion), channel_id=1, source_target_pairs={{0,256},{16,272},{32,288},{48,304},{64,320},{80,336},{96,352},{112... | collective-permute-start | bytes 104456 | tf_op jit(solution)/shard_map/ppermute | solution.py:13
  85.2 5.6 %collective-permute-start.3 = (bf16[136,128]{1,0:T(8,128)(2,1)S(1)}, bf16[136,128]{1,0:T(8,128)(2,1)S(1)}, u32[]{:S(2)}, u32[]{:S(2)}) collective-permute-start(bf16[136,128]{1,0:T(8,128)(2,1)S(1)} %pad_maximum_fusion), channel_id=1, source_target_pairs={{0,384},{16,400},{32,416},{48,432},{64,448},{80,464},{96,480},{112... | collective-permute-start | bytes 104456 | tf_op jit(solution)/shard_map/ppermute | solution.py:13
  96.6 12.7 %all-to-all-start.2 = ((bf16[8,128,128]{2,1,0:T(8,128)(2,1)}), bf16[8,128,128]{2,1,0:T(8,128)(2,1)S(1)}, u32[]{:S(2)}, u32[]{:S(2)}) async-start(bf16[8,128,128]{2,1,0:T(8,128)(2,1)} %constant_dynamic-update-slice_fusion.16), calls=%async_computation.2 | async-start | bytes 524288 | tf_op jit(solution)/shard_map/all_to_all | solution.py:87
  103.1 6.2 %copy-start.2 = (f32[8,128]{1,0:T(8,128)S(1)}, f32[8,128]{1,0:T(8,128)}, u32[]{:S(2)}) copy-start(f32[8,128]{1,0:T(8,128)} %mul.666) | copy-start | bytes 12292
  112.3 2.4 %copy-start.1 = (bf16[1024,512]{1,0:T(8,128)(2,1)S(1)}, bf16[1024,512]{1,0:T(8,128)(2,1)}, u32[]{:S(2)}) copy-start(bf16[1024,512]{1,0:T(8,128)(2,1)} %param.23) | copy-start | bytes 3145732
  112.3 2.4 %copy-start.5 = (f32[1024]{0:T(1024)S(1)}, f32[1024]{0:T(1024)}, u32[]{:S(2)}) copy-start(f32[1024]{0:T(1024)} %param.22) | copy-start | bytes 12292
